TPU v7x, 256 devices: a whole 4x4x8 slice. The times are simulated.
256 devices in a mesh: probe: 64 (over z, x_lo, y), slab: 4 (over x_hi, core).
Axes of the slice: x: 4 (x_hi: 2, x_lo: 2; x = x_hi * 2 + x_lo), y: 4, z: 8, core: 2. Of those that a mesh axis runs over, the one named last changes fastest.
Arguments:
- smatrix: bfloat16 [2, 512, 128, 128], P(None, 'probe', 'slab'), may hold values from -6 to 6
- amplitude: float32 [2, 512], replicated, may hold values from -0.25 to 0.25
- beam_index: int32 [512, 2], replicated, may hold values from -32 to 31
- positions: int32 [8192, 2], P('probe'), may hold values from -8 to 8
Outputs:
- patterns: float32 [8192, 128, 128], P('probe', 'slab')
Inputs may be any that keep to these rules, and one draw needn't show every extreme that they name: `positions`: column 0 is the row offset that places a probe's crop in the band, column 1 the column offset. `beam_index`: column 0 along rows, column 1 along columns.
All inputs are finite; a program needn't handle non-finite values.
Results may differ from a plain program's by a relative error of at most 0.0029.
Values may be sent and summed in bfloat16 or wider, within the bound.
A program may use at most 128 MiB of HBM per device.

v0:
```python
import math
import jax
import jax.numpy as jnp
from jax import lax
from jax.sharding import PartitionSpec as P

HALO = 8
SIDE = 2 * HALO + 1
SPOTS = SIDE * SIDE


def dft_table(first, second, length):
    angle = (
        2.0
        * math.pi
        * (jnp.mod(first[:, None] * second[None, :], length).astype(jnp.float32) / length)
    )
    return (jnp.cos(angle), jnp.sin(angle))


def spot_weights(amplitude, beam_index, rows_all, cols):
    spot = jnp.arange(SPOTS, dtype=jnp.int32)
    row, col = (spot // SIDE - HALO, spot % SIDE - HALO)
    turn = jnp.mod(beam_index[:, 0:1] * row[None, :], rows_all).astype(jnp.float32) / rows_all
    turn = turn + jnp.mod(beam_index[:, 1:2] * col[None, :], cols).astype(jnp.float32) / cols
    cosine, sine = (jnp.cos(2.0 * math.pi * turn), jnp.sin(2.0 * math.pi * turn))
    re, im = (amplitude[0][:, None], amplitude[1][:, None])
    return (
        (re * cosine + im * sine).astype(jnp.bfloat16),
        (im * cosine - re * sine).astype(jnp.bfloat16),
    )


def on_device(smatrix, amplitude, beam_index, positions):
    _, beams_here, slab_rows, cols = smatrix.shape
    groups = lax.axis_size("probe")
    slabs = lax.axis_size("slab")
    rows_all = slab_rows * slabs
    own = cols // groups
    highest = lax.Precision.HIGHEST
    f32 = jnp.float32
    index = jnp.arange(cols, dtype=jnp.int32)
    cos, sin = dft_table(index, index, cols)
    cos, sin = (cos / math.sqrt(cols), sin / math.sqrt(cols))
    s_re, s_im = (smatrix[0].astype(f32), smatrix[1].astype(f32))
    mm = lambda a, b: jnp.einsum("lc,brc->lbr", a, b, precision=highest)
    half = jnp.stack([mm(cos, s_re) + mm(sin, s_im), mm(cos, s_im) - mm(sin, s_re)], 1)
    half = half.astype(jnp.bfloat16).reshape(groups, own, 2, beams_here, slab_rows)
    got = lax.all_to_all(half, "probe", split_axis=0, concat_axis=0, tiled=True)
    got = lax.all_gather(got, "slab", axis=0)
    got = jnp.transpose(got, (2, 0, 5, 3, 1, 4)).reshape(own, rows_all, 2, groups * beams_here)
    w_re, w_im = spot_weights(amplitude, beam_index, rows_all, cols)
    field = jnp.concatenate([got[:, :, 0], got[:, :, 1]], axis=-1)
    u_re = jnp.dot(field, jnp.concatenate([w_re, -w_im], 0), preferred_element_type=f32)
    u_im = jnp.dot(field, jnp.concatenate([w_im, w_re], 0), preferred_element_type=f32)
    row = jnp.arange(rows_all, dtype=jnp.int32)[:, None]
    shift = (jnp.arange(SPOTS, dtype=jnp.int32) // SIDE - HALO)[None, :]
    inside = (row >= shift) & (row < rows_all + shift)
    u_re = jnp.where(inside[None], u_re, 0.0)
    u_im = jnp.where(inside[None], u_im, 0.0)
    freq = lax.axis_index("slab") * slab_rows + jnp.arange(slab_rows, dtype=jnp.int32)
    rcos, rsin = dft_table(freq, row[:, 0], rows_all)
    rcos, rsin = (rcos / math.sqrt(rows_all), rsin / math.sqrt(rows_all))
    mm = lambda a, b: jnp.einsum("kr,lrs->lks", a, b, precision=highest)
    out_re = mm(rcos, u_re) + mm(rsin, u_im)
    out_im = mm(rcos, u_im) - mm(rsin, u_re)
    power = (out_re**2 + out_im**2).astype(jnp.bfloat16)
    table = lax.all_gather(power, "probe", axis=0, tiled=True)
    spot = (positions[:, 0] + HALO) * SIDE + positions[:, 1] + HALO
    pick = (spot[:, None] == jnp.arange(SPOTS, dtype=jnp.int32)[None, :]).astype(jnp.bfloat16)
    return jnp.einsum("ps,lks->pkl", pick, table, preferred_element_type=f32)


def solution(mesh):
    return jax.shard_map(
        on_device,
        mesh=mesh,
        in_specs=(P(None, "probe", "slab", None), P(), P(), P("probe", None)),
        out_specs=P("probe", "slab", None),
        check_vma=False,
    )
```

profile of v0, /device:TPU:4, one launch (start us, length us, event | category | flops | bytes accessed | tf_op | source)
XLA Modules:
  0.0 372.4 jit_solution(1641833828458793947)
XLA Ops:
  6.5 0.0 copy-start
  6.5 0.0 copy-start.1
  6.5 1.3 fusion.31
  7.9 1.3 fusion.37
  9.2 1.3 fusion.6
  10.5 1.3 fusion.5
  11.9 0.2 copy.21
  12.1 0.2 copy.22
  12.2 0.1 copy_bitcast_fusion.1
  12.4 1.1 reshape.91
  13.4 12.7 %all-to-all-start = ((bf16[64,2,512]{2,1,0:T(2,128)(2,1)}), bf16[64,2,512]{2,1,0:T(2,128)(2,1)S(1)}, u32[]{:S(2)}, u32[]{:S(2)}) async-start(bf16[64,2,512]{2,1,0:T(2,128)(2,1)} %reshape.91), calls=%async_computation | async-start | bytes 262144 | tf_op jit(solution)/shard_map/all_to_all | solution.py:49
  26.2 0.0 all-gather.3.cloned.1.call-start
  26.3 0.0 copy-done
  26.3 0.0 copy-done.1
  26.3 0.1 fusion.24
  26.5 3.6 fusion.126
  30.1 2.9 subtract_convert_fusion
  33.0 4.1 %all-to-all-done = bf16[64,2,512]{2,1,0:T(2,128)(2,1)S(1)} async-done(((bf16[64,2,512]{2,1,0:T(2,128)(2,1)}), bf16[64,2,512]{2,1,0:T(2,128)(2,1)S(1)}, u32[]{:S(2)}, u32[]{:S(2)}) %all-to-all-start) | async-done | bytes 131104 | tf_op jit(solution)/shard_map/all_to_all | solution.py:49
  37.1 0.3 reshape.92
  37.4 0.1 copy.24
  37.5 15.7 %all-gather = bf16[256,2,2,8,32]{4,3,2,1,0:T(8,128)(2,1)S(1)} all-gather(bf16[64,2,2,8,32]{4,3,2,1,0:T(8,128)(2,1)S(1)} %copy.24), channel_id=2, replica_groups=mesh['probe'=64,'slab'=4] {'slab'}, dimensions={0}, use_global_device_ids=true | all-gather | bytes 655360 | tf_op jit(solution)/shard_map/all_gather | solution.py:50
  53.2 2.7 copy.38
  55.9 1.1 reshape.82
  56.9 0.0 copy-start.3
  57.0 0.1 copy.30
  57.1 0.1 copy.31
  57.3 0.4 convolution_select_fusion
  57.7 0.2 copy-done.3
  57.9 0.0 copy-start.2
  57.9 0.4 convolution_select_fusion.1
  58.3 0.6 fusion.63
  58.9 0.6 fusion.61
  59.5 0.6 fusion.9
  60.1 1.2 fusion.11
  61.3 0.0 all-gather.3.cloned.1.call-update
  61.3 0.0 copy-done.2
  61.4 298.6 %all-gather.3.cloned.1.call-done = bf16[128,32,289]{2,1,0:T(8,128)(2,1)} async-done(((bf16[2,32,289]{2,1,0:T(8,128)(2,1)}), bf16[128,32,289]{2,1,0:T(8,128)(2,1)}) %all-gather.3.cloned.1.call-update) | async-done | bytes 2367504 | tf_op jit(solution)/shard_map/all_gather | solution.py:68
  359.9 3.6 fusion.2
  363.6 2.0 copy.29
  (7 shorter events, 0.1 us)
Async XLA Ops:
  6.5 19.8 %copy-start = (f32[2,512]{1,0:T(2,128)S(1)}, f32[2,512]{1,0:T(2,128)}, u32[]{:S(2)}) copy-start(f32[2,512]{1,0:T(2,128)} %param.5) | copy-start | bytes 12292
  6.5 19.8 %copy-start.1 = (s32[512,2]{0,1:T(2,128)S(1)}, s32[512,2]{0,1:T(2,128)}, u32[]{:S(2)}) copy-start(s32[512,2]{0,1:T(2,128)} %param.6) | copy-start | bytes 12292
  13.4 23.7 %all-to-all-start = ((bf16[64,2,512]{2,1,0:T(2,128)(2,1)}), bf16[64,2,512]{2,1,0:T(2,128)(2,1)S(1)}, u32[]{:S(2)}, u32[]{:S(2)}) async-start(bf16[64,2,512]{2,1,0:T(2,128)(2,1)} %reshape.91), calls=%async_computation | async-start | bytes 262144 | tf_op jit(solution)/shard_map/all_to_all | solution.py:49
  26.2 333.8 %all-gather.3.cloned.1.call-start = ((), (), s32[]{:S(2)}) async-start(), calls=%async_computation.1 | async-start | bytes 3194880 | tf_op jit(solution)/shard_map/all_gather | solution.py:68
  56.9 1.0 copy-start.3
  57.9 3.5 copy-start.2
Sparse Core Ops, SparseCore 0:
  61.5 298.4 all-gather.2
where the time goes:
time: 373 us; the launch traced here: 372 us
  waiting for transfers between devices  303 us (81%)
  blocking collectives  15.7 us (4%)
  between operations  13.6 us (4%)
  starting transfers between devices  12.8 us (3%)
  matrix products  12.7 us (3%)
  local copies, waits for them, and re-layouts  8.13 us (2%)
  other arithmetic  6.82 us (2%)
    all_gather x1, waiting for transfers between devices, on_device(): table = lax.all_gather(power, 'probe', axis=0, tiled=True)  299 us
    all_gather x1, blocking collectives, on_device(): got = lax.all_gather(got, 'slab', axis=0)  15.7 us
    all_to_all x1, starting transfers between devices, on_device(): got = lax.all_to_all(half, 'probe', split_axis=0, concat_axis=0, tiled=True)  12.7 us
  transfers between devices with their start and end apart: 2, of which 2 were waited for; matrix products, arithmetic and copies ran while one was open for 2% of the time, Pallas kernels for 0%

commit v1 on v0

--- a/solution.py
+++ b/solution.py
@@ -65,7 +65,9 @@
     out_re = mm(rcos, u_re) + mm(rsin, u_im)
     out_im = mm(rcos, u_im) - mm(rsin, u_re)
     power = (out_re**2 + out_im**2).astype(jnp.bfloat16)
-    table = lax.all_gather(power, "probe", axis=0, tiled=True)
+    table = jnp.concatenate(
+        lax.all_to_all(jnp.stack([power] * lax.axis_size("probe")), "probe", 0, 0), axis=0
+    )
     spot = (positions[:, 0] + HALO) * SIDE + positions[:, 1] + HALO
     pick = (spot[:, None] == jnp.arange(SPOTS, dtype=jnp.int32)[None, :]).astype(jnp.bfloat16)
     return jnp.einsum("ps,lks->pkl", pick, table, preferred_element_type=f32)

time: 373 us -> 145 us (0.39)
  waiting for transfers between devices: 303 us -> 77.5 us
  between operations: 13.6 us -> 0.26 us
  starting transfers between devices: 12.8 us -> 20.7 us
    all_gather x1 -> x0, waiting for transfers between devices: 299 us -> none  [on_device(): table = lax.all_gather(power, 'probe', axis=0, tiled=True)]
    all_to_all x0 -> x1, waiting for transfers between devices: none -> 73.4 us  [on_device(): lax.all_to_all(jnp.stack([power] * lax.axis_size('probe')), 'probe', 0, 0)]
    all_to_all x0 -> x1, starting transfers between devices: none -> 8 us  [on_device(): lax.all_to_all(jnp.stack([power] * lax.axis_size('probe')), 'probe', 0, 0)]
  transfers between devices with their start and end apart: 2 -> 2, of which waited for: 2 -> 2; matrix products, arithmetic and copies ran while one was open for 2% -> 5% of each run, Pallas kernels for 0% -> 0%
where the time goes in v1:
time: 145 us; the launch traced here: 144 us
  waiting for transfers between devices  77.5 us (53%)
  starting transfers between devices  20.7 us (14%)
  blocking collectives  15.7 us (11%)
  local copies, waits for them, and re-layouts  11.7 us (8%)
  matrix products  11.5 us (8%)
  other arithmetic  6.82 us (5%)
    all_to_all x1, waiting for transfers between devices, on_device(): lax.all_to_all(jnp.stack([power] * lax.axis_size('probe')), 'probe', 0, 0)  73.4 us
    all_gather x1, blocking collectives, on_device(): got = lax.all_gather(got, 'slab', axis=0)  15.7 us
    all_to_all x1, starting transfers between devices, on_device(): got = lax.all_to_all(half, 'probe', split_axis=0, concat_axis=0, tiled=True)  12.7 us
    all_to_all x1, starting transfers between devices, on_device(): lax.all_to_all(jnp.stack([power] * lax.axis_size('probe')), 'probe', 0, 0)  8 us
    dot_general x4, matrix products, on_device(): mm = lambda a, b: jnp.einsum('lc,brc->lbr', a, b, precision=highest)  5.29 us
    all_to_all x1, waiting for transfers between devices, on_device(): got = lax.all_to_all(half, 'probe', split_axis=0, concat_axis=0, tiled=True)  4.12 us
    neg x1, other arithmetic, on_device(): -w_im  3.6 us
    dot_general x1, matrix products, on_device(): return jnp.einsum('ps,lks->pkl', pick, table, preferred_element_type=f32)  3.1 us
  transfers between devices with their start and end apart: 2, of which 2 were waited for; matrix products, arithmetic and copies ran while one was open for 5% of the time, Pallas kernels for 0%

profile of v1, /device:TPU:4, one launch (start us, length us, event | category | flops | bytes accessed | tf_op | source)
XLA Modules:
  0.0 144.3 jit_solution(3149367713366920787)
XLA Ops:
  0.0 0.0 copy-start
  0.0 0.0 copy-start.1
  0.0 1.3 fusion.37
  1.3 1.3 fusion.31
  2.7 1.3 fusion.5
  4.0 0.2 copy.23
  4.2 1.3 fusion.6
  5.5 0.2 copy.24
  5.7 0.1 copy_bitcast_fusion.1
  5.8 1.1 reshape.97
  6.9 12.7 %all-to-all-start = ((bf16[64,2,512]{2,1,0:T(2,128)(2,1)}), bf16[64,2,512]{2,1,0:T(2,128)(2,1)S(1)}, u32[]{:S(2)}, u32[]{:S(2)}) async-start(bf16[64,2,512]{2,1,0:T(2,128)(2,1)} %reshape.97), calls=%async_computation | async-start | bytes 262144 | tf_op jit(solution)/shard_map/all_to_all | solution.py:49
  19.7 0.0 copy-done
  19.7 0.0 copy-done.1
  19.7 0.1 fusion.24
  19.9 3.6 %fusion.126 = bf16[512,289]{0,1:T(8,128)(2,1)} fusion(f32[512]{0:T(512)S(1)} %bitcast.79, s32[289]{0:T(512)S(1)} %get-tuple-element.13, s32[512]{0:T(512)S(1)} %bitcast.83, s32[289]{0:T(512)S(1)} %get-tuple-element.14, s32[512]{0:T(512)S(1)} %bitcast.81, f32[512]{0:T(512)S(1)} %bitcast.77), kind=kLoop, calls=%fused_computation.159 | loop fusion | flops 5178880 | bytes 306440 | tf_op jit(solution)/shard_map/neg | solution.py:54
  23.5 2.9 %subtract_convert_fusion = (bf16[512,289]{0,1:T(8,128)(2,1)S(1)}, bf16[512,289]{0,1:T(8,128)(2,1)S(1)}) fusion(f32[512]{0:T(512)S(1)} %bitcast.78, s32[289]{0:T(512)S(1)} %get-tuple-element.13, s32[512]{0:T(512)S(1)} %bitcast.84, s32[289]{0:T(512)S(1)} %get-tuple-element.14, s32[512]{0:T(512)S(1)} %bitcast.82, f32[512]{0:T(512)S(1)} %bitcast.80), kind=kLoop, calls=%fused_computation.39 | loop fusion | flops 5326848 | bytes 602376 | tf_op jit(solution)/shard_map/convert_element_type | solution.py:30
  26.4 4.1 %all-to-all-done = bf16[64,2,512]{2,1,0:T(2,128)(2,1)S(1)} async-done(((bf16[64,2,512]{2,1,0:T(2,128)(2,1)}), bf16[64,2,512]{2,1,0:T(2,128)(2,1)S(1)}, u32[]{:S(2)}, u32[]{:S(2)}) %all-to-all-start) | async-done | bytes 131104 | tf_op jit(solution)/shard_map/all_to_all | solution.py:49
  30.6 0.3 reshape.98
  30.8 0.1 copy.26
  30.9 15.7 %all-gather = bf16[256,2,2,8,32]{4,3,2,1,0:T(8,128)(2,1)S(1)} all-gather(bf16[64,2,2,8,32]{4,3,2,1,0:T(8,128)(2,1)S(1)} %copy.26), channel_id=2, replica_groups=mesh['probe'=64,'slab'=4] {'slab'}, dimensions={0}, use_global_device_ids=true | all-gather | bytes 655360 | tf_op jit(solution)/shard_map/all_gather | solution.py:50
  46.6 2.7 %copy.40 = bf16[4,64,2,2,8,32]{5,0,4,1,3,2:T(4,128)(2,1)S(1)} copy(bf16[4,64,2,2,8,32]{5,4,3,2,1,0:T(8,128)(2,1)S(1)} %bitcast.68) | data formatting | bytes 1048576 | tf_op jit(solution)/shard_map/all_gather | solution.py:50
  49.3 1.1 reshape.87
  50.4 0.0 copy-start.3
  50.4 0.1 copy.32
  50.6 0.1 copy.33
  50.7 0.6 copy-done.3
  51.3 0.4 convolution_select_fusion.1
  51.7 0.4 convolution_select_fusion
  52.1 0.6 fusion.63
  52.7 0.6 fusion.61
  53.3 0.6 fusion.9
  53.9 0.6 fusion.11
  54.5 2.1 %stack.11 = bf16[64,2,32,289]{3,2,1,0:T(8,128)(2,1)} broadcast(bf16[2,32,289]{2,1,0:T(8,128)(2,1)S(1)} %fusion.11), dimensions={1,2,3} | broadcast | bytes 2404480 | tf_op jit(solution)/shard_map/stack | solution.py:69
  56.7 0.0 copy-start.2
  56.7 8.0 %all-to-all-start.1 = ((bf16[64,2,32,289]{3,2,1,0:T(8,128)(2,1)}), bf16[64,2,32,289]{3,2,1,0:T(8,128)(2,1)S(1)}, u32[]{:S(2)}, u32[]{:S(2)}) async-start(bf16[64,2,32,289]{3,2,1,0:T(8,128)(2,1)} %stack.11), calls=%async_computation.1 | async-start | bytes 6291456 | tf_op jit(solution)/shard_map/all_to_all | solution.py:69
  64.7 0.0 copy-done.2
  64.7 73.4 %all-to-all-done.1 = bf16[64,2,32,289]{3,2,1,0:T(8,128)(2,1)S(1)} async-done(((bf16[64,2,32,289]{3,2,1,0:T(8,128)(2,1)}), bf16[64,2,32,289]{3,2,1,0:T(8,128)(2,1)S(1)}, u32[]{:S(2)}, u32[]{:S(2)}) %all-to-all-start.1) | async-done | bytes 2367520 | tf_op jit(solution)/shard_map/all_to_all | solution.py:69
  138.1 3.1 %fusion.2 = f32[128,32,128]{0,2,1:T(8,128)} fusion(bf16[128,32,289]{2,1,0:T(8,128)(2,1)S(1)} %bitcast.67, s32[128]{0:T(128)S(1)} %add_bitcast_fusion), kind=kOutput, calls=%fused_computation.3 | convolution fusion | flops 303075456 | bytes 4465152 | tf_op jit(solution)/shard_map/ps,lks->pkl/dot_general | solution.py:73
  141.2 3.0 %copy.31 = f32[128,32,128]{2,1,0:T(8,128)} copy(f32[128,32,128]{0,2,1:T(8,128)} %fusion.2) | data formatting | bytes 4194304 | tf_op jit(solution)/shard_map/ps,lks->pkl/transpose | solution.py:73
  (7 shorter events, 0.1 us)
Async XLA Ops:
  0.0 19.7 %copy-start = (f32[2,512]{1,0:T(2,128)S(1)}, f32[2,512]{1,0:T(2,128)}, u32[]{:S(2)}) copy-start(f32[2,512]{1,0:T(2,128)} %param.5) | copy-start | bytes 12292
  0.0 19.7 %copy-start.1 = (s32[512,2]{0,1:T(2,128)S(1)}, s32[512,2]{0,1:T(2,128)}, u32[]{:S(2)}) copy-start(s32[512,2]{0,1:T(2,128)} %param.6) | copy-start | bytes 12292
  6.9 23.7 %all-to-all-start = ((bf16[64,2,512]{2,1,0:T(2,128)(2,1)}), bf16[64,2,512]{2,1,0:T(2,128)(2,1)S(1)}, u32[]{:S(2)}, u32[]{:S(2)}) async-start(bf16[64,2,512]{2,1,0:T(2,128)(2,1)} %reshape.97), calls=%async_computation | async-start | bytes 262144 | tf_op jit(solution)/shard_map/all_to_all | solution.py:49
  50.4 1.0 copy-start.3
  56.7 8.0 %copy-start.2 = (s32[128,2]{0,1:T(2,128)S(1)}, s32[128,2]{0,1:T(2,128)}, u32[]{:S(2)}) copy-start(s32[128,2]{0,1:T(2,128)} %param.7) | copy-start | bytes 3076
  56.7 81.4 %all-to-all-start.1 = ((bf16[64,2,32,289]{3,2,1,0:T(8,128)(2,1)}), bf16[64,2,32,289]{3,2,1,0:T(8,128)(2,1)S(1)}, u32[]{:S(2)}, u32[]{:S(2)}) async-start(bf16[64,2,32,289]{3,2,1,0:T(8,128)(2,1)} %stack.11), calls=%async_computation.1 | async-start | bytes 6291456 | tf_op jit(solution)/shard_map/all_to_all | solution.py:69
